TPU v7x, 32 devices: a whole 2x2x4 slice. The times are simulated.
32 devices in a mesh: groups: 2 (over y), ctx: 4 (over x, core), mp: 4 (over z).
Axes of the slice: x: 2, y: 2, z: 4, core: 2. Of those that a mesh axis runs over, the one named last changes fastest.
Arguments:
- tokens: bfloat16 [3072, 8192], P(('groups', 'ctx')), parts along dimension 0, may hold values from -6 to 6
- norm_gain: bfloat16 [8192], replicated, may hold values from 0.099609375 to 1.8984375
- w_query: bfloat16 [8192, 4096], P('ctx', 'mp'), may hold values from -0.44194174 to 0.44194174
- w_key: bfloat16 [8192, 1024], P('ctx', 'mp'), may hold values from -0.044194174 to 0.044194174
- value_weight: bfloat16 [8192, 1024], P('ctx', 'mp'), may hold values from -0.0625 to 0.0625
- slab_order: int32 [8], P('groups'), parts along dimension 0, may hold values from 0 to 3, each once
- segment_ids: int32 [3072], P('groups'), parts along dimension 0, may hold values from 0 to 3, as said below
Outputs:
- attended: bfloat16 [3072, 4096], P(('groups', 'ctx'), 'mp'), parts along dimension 0
There are 2 independent parts, one for each index of `groups`. A program takes and returns all parts, laid end to end along the dimension named above; an argument that names none is the same for every part. Nothing has to cross between parts.
Inputs may be any that keep to these rules, and one draw needn't show every extreme that they name: `segment_ids`: never falling along positions; each of the 4 segments holds at least one position.
All inputs are finite; a program needn't handle non-finite values.
Results may differ from a plain program's by a relative error of at most 0.012.
Values may be sent and summed in bfloat16 or wider, within the bound.
A program may use at most 128 MiB of HBM per device.

v0:
```python
import math
import jax
import jax.numpy as jnp
from jax import lax
from jax.sharding import PartitionSpec as P

HEAD_SIZE = 128


def apply_rotary(values, positions, heads):
    width = values.shape[1] // heads
    half = width // 2
    freqs = jnp.exp(jnp.arange(half, dtype=jnp.float32) * (-2.0 * math.log(500000.0) / width))
    angles = positions.astype(jnp.float32)[:, None] * freqs[None, :]
    cosine = jnp.cos(angles)[:, None, :]
    sine = jnp.sin(angles)[:, None, :]
    shaped = values.reshape(values.shape[0], heads, width)
    first = shaped[..., :half]
    second = shaped[..., half:]
    turned = jnp.concatenate(
        [first * cosine - second * sine, second * cosine + first * sine], axis=-1
    )
    return turned.reshape(values.shape)


def local(tokens, norm_gain, w_query, w_key, value_weight, slab_order, segment_ids):
    tok_rows = tokens.shape[0]
    device_slab = lax.axis_index("ctx")
    position_all = (
        slab_order[:, None] * tok_rows + jnp.arange(tok_rows, dtype=jnp.int32)[None, :]
    ).reshape(-1)
    segment_all = jnp.take(segment_ids, position_all)
    my_position = lax.dynamic_slice_in_dim(position_all, device_slab * tok_rows, tok_rows)
    my_segment = lax.dynamic_slice_in_dim(segment_all, device_slab * tok_rows, tok_rows)
    floats = tokens.astype(jnp.float32)
    inverse = lax.rsqrt(jnp.mean(floats * floats, axis=-1, keepdims=True) + 1e-05)
    normed = (floats * inverse * norm_gain.astype(jnp.float32)[None, :]).astype(jnp.bfloat16)
    query_cols = w_query.shape[1]
    key_cols = w_key.shape[1]
    query = jnp.dot(
        normed,
        lax.all_gather(w_query, "ctx", axis=0, tiled=True),
        preferred_element_type=jnp.float32,
    )
    key_projected = jnp.dot(
        normed, lax.all_gather(w_key, "ctx", axis=0, tiled=True), preferred_element_type=jnp.float32
    )
    value_proj = jnp.dot(
        normed,
        lax.all_gather(value_weight, "ctx", axis=0, tiled=True),
        preferred_element_type=jnp.float32,
    )
    head_size = HEAD_SIZE
    heads_here = query_cols // head_size
    kv_here = key_cols // head_size
    group_width = heads_here // kv_here
    query_rot = (
        apply_rotary(query, my_position, heads_here)
        .astype(jnp.bfloat16)
        .reshape(tok_rows, kv_here, group_width, head_size)
    )
    key_rotary = apply_rotary(key_projected, my_position, kv_here).astype(jnp.bfloat16)
    value_b = value_proj.astype(jnp.bfloat16)
    scale = head_size ** (-0.5)
    start_state = (
        jnp.full((kv_here, group_width, tok_rows), -1e30, jnp.float32),
        jnp.zeros((kv_here, group_width, tok_rows), jnp.float32),
        jnp.zeros((kv_here, group_width, tok_rows, head_size), jnp.float32),
    )
    state = start_state
    key_piece = lax.all_gather(key_rotary, "ctx", axis=0, tiled=True)
    value_piece = lax.all_gather(value_b, "ctx", axis=0, tiled=True)
    piece_rows = key_piece.shape[0]
    block_rows = math.gcd(piece_rows, 1024)
    block_count = piece_rows // block_rows
    key_blocks = key_piece.reshape(block_count, block_rows, kv_here, head_size)
    value_blocks = value_piece.reshape(block_count, block_rows, kv_here, head_size)
    key_positions = position_all.reshape(block_count, block_rows)
    key_segments = segment_all.reshape(block_count, block_rows)

    def advance(inner, item):
        key_block, value_block, block_positions, block_segments = item
        allowed = (block_positions[None, :] <= my_position[:, None]) & (
            block_segments[None, :] == my_segment[:, None]
        )
        running_max, running_sum, running_acc = inner
        scores = (
            jnp.einsum("tkgd,nkd->kgtn", query_rot, key_block, preferred_element_type=jnp.float32)
            * scale
        )
        scores = jnp.where(allowed[None, None], scores, -1e30)
        new_max = jnp.maximum(running_max, jnp.max(scores, axis=-1))
        exps = jnp.where(allowed[None, None], jnp.exp(scores - new_max[..., None]), 0.0)
        factor = jnp.exp(running_max - new_max)
        new_sum = running_sum * factor + jnp.sum(exps, axis=-1)
        new_acc = running_acc * factor[..., None] + jnp.einsum(
            "kgtn,nkd->kgtd",
            exps.astype(jnp.bfloat16),
            value_block,
            preferred_element_type=jnp.float32,
        )
        inner = (new_max, new_sum, new_acc)
        return (inner, None)

    state, _ = lax.scan(advance, state, (key_blocks, value_blocks, key_positions, key_segments))
    final_max, final_sum, final_acc = state
    mixed = final_acc / final_sum[..., None]
    return (
        jnp.transpose(mixed, (2, 0, 1, 3))
        .reshape(tok_rows, heads_here * head_size)
        .astype(jnp.bfloat16)
    )


def solution(mesh):
    return jax.shard_map(
        local,
        mesh=mesh,
        in_specs=(
            P(("groups", "ctx"), None),
            P(),
            P("ctx", "mp"),
            P("ctx", "mp"),
            P("ctx", "mp"),
            P("groups"),
            P("groups"),
        ),
        out_specs=P(("groups", "ctx"), "mp"),
        check_vma=False,
    )
```

profile of v0, /device:TPU:0, one launch (start us, length us, event | category | flops | bytes accessed | tf_op | source)
XLA Modules:
  0.0 256.6 jit_solution(9475699111471552098)
XLA Ops:
  6.5 0.0 copy-start
  6.5 0.0 copy-start.3
  6.5 0.0 copy-start.2
  6.5 0.0 all-gather.4.cloned.1.call-start
  6.5 0.7 all-gather.4.cloned.1.call-update
  7.3 0.0 all-gather.8.cloned.1.call-start
  7.3 0.7 all-gather.8.cloned.1.call-update
  8.0 0.0 all-gather.6.cloned.1.call-start
  8.1 0.7 all-gather.6.cloned.1.call-update
  8.8 0.0 copy-done.3
  8.8 0.1 fusion.19
  8.9 0.1 fusion.24
  9.0 0.4 multiply_cosine_fusion
  9.4 0.1 copy.16
  9.6 0.1 copy.17
  9.7 0.0 copy-done.2
  9.8 0.0 copy-done
  9.8 8.4 %gather_fusion = s32[1536]{0:T(1024)S(1)} fusion(s32[1536]{0:T(1024)S(1)} %copy-done, s32[2048]{0:T(1024)S(1)} %pad_clamp_fusion), kind=kCustom, calls=%fused_computation | custom fusion | bytes 18432 | tf_op jit(solution)/shard_map/jit(_take)/gather | solution.py:32
  18.2 5.0 %fusion.14 = f32[384]{0:T(512)S(1)} fusion(bf16[384,8192]{1,0:T(8,128)(2,1)} %param.9), kind=kLoop, calls=%fused_computation.27 | loop fusion | flops 9436800 | bytes 6292992 | tf_op jit(solution)/shard_map/reduce_sum | solution.py:36
  23.2 0.1 dynamic-slice_select_fusion
  23.3 22.8 %all-gather.4.cloned.1.call-done = bf16[8192,256]{1,0:T(8,128)(2,1)} async-done(((bf16[2048,256]{1,0:T(8,128)(2,1)}), bf16[8192,256]{1,0:T(8,128)(2,1)}) %all-gather.4.cloned.1.call-update) | async-done | bytes 4194320 | tf_op jit(solution)/shard_map/all_gather | solution.py:46
  46.1 6.6 %fusion.22 = f32[384,256]{0,1:T(8,128)S(1)} fusion(bf16[8192,256]{1,0:T(8,128)(2,1)} %all-gather.4.cloned.1.call-done, bf16[384,8192]{1,0:T(8,128)(2,1)} %param.9, f32[8192]{0:T(1024)S(1)} %convert_element_type.38, f32[384]{0:T(512)S(1)} %add_rsqrt_fusion), kind=kOutput, calls=%fused_computation.54 | convolution fusion | flops 1623195648 | bytes 10913280 | tf_op jit(solution)/shard_map/dot_general | solution.py:45
  52.8 0.1 subtract_convert_fusion.1
  52.8 0.1 copy.25
  53.0 11.9 %all_gather.16 = bf16[1536,256]{1,0:T(8,128)(2,1)S(1)} all-gather(bf16[384,256]{1,0:T(8,128)(2,1)S(1)} %copy.25), channel_id=1, replica_groups=mesh['groups'=2,'ctx'=4,'mp'=4] {'ctx'}, dimensions={0}, use_global_device_ids=true | all-gather | bytes 983040 | tf_op jit(solution)/shard_map/all_gather | solution.py:71
  64.9 0.2 reshape.188
  65.1 19.7 %all-gather.8.cloned.1.call-done = bf16[8192,256]{1,0:T(8,128)(2,1)} async-done(((bf16[2048,256]{1,0:T(8,128)(2,1)}), bf16[8192,256]{1,0:T(8,128)(2,1)}) %all-gather.8.cloned.1.call-update) | async-done | bytes 4194320 | tf_op jit(solution)/shard_map/all_gather | solution.py:50
  84.8 5.9 %convolution_convert_fusion = bf16[384,256]{1,0:T(8,128)(2,1)S(1)} fusion(bf16[8192,256]{1,0:T(8,128)(2,1)} %all-gather.8.cloned.1.call-done, bf16[384,8192]{1,0:T(8,128)(2,1)} %param.9, f32[8192]{0:T(1024)S(1)} %convert_element_type.38, f32[384]{0:T(512)S(1)} %add_rsqrt_fusion), kind=kOutput, calls=%fused_computation.34 | convolution fusion | flops 1623293952 | bytes 10716672 | tf_op jit(solution)/shard_map/dot_general | solution.py:48
  90.7 8.8 %all_gather.19 = bf16[1536,256]{1,0:T(8,128)(2,1)S(1)} all-gather(bf16[384,256]{1,0:T(8,128)(2,1)S(1)} %convolution_convert_fusion), channel_id=1, replica_groups=mesh['groups'=2,'ctx'=4,'mp'=4] {'ctx'}, dimensions={0}, use_global_device_ids=true | all-gather | bytes 983040 | tf_op jit(solution)/shard_map/all_gather | solution.py:72
  99.5 0.2 reshape.190
  99.7 92.7 %all-gather.6.cloned.1.call-done = bf16[8192,1024]{1,0:T(8,128)(2,1)} async-done(((bf16[2048,1024]{1,0:T(8,128)(2,1)}), bf16[8192,1024]{1,0:T(8,128)(2,1)}) %all-gather.6.cloned.1.call-update) | async-done | bytes 16777232 | tf_op jit(solution)/shard_map/all_gather | solution.py:42
  192.3 12.4 %convolution_bitcast_fusion = f32[48,8,8,128]{3,1,2,0:T(8,128)S(1)} fusion(bf16[8192,1024]{1,0:T(8,128)(2,1)} %all-gather.6.cloned.1.call-done, bf16[384,8192]{1,0:T(8,128)(2,1)} %param.9, f32[8192]{0:T(1024)S(1)} %convert_element_type.38, f32[384]{0:T(512)S(1)} %add_rsqrt_fusion), kind=kOutput, calls=%fused_computation.33 | convolution fusion | flops 6455033856 | bytes 24675840 | tf_op jit(solution)/shard_map/dot_general | solution.py:40
  204.7 0.3 copy.29
  205.1 0.7 subtract_convert_fusion
  205.7 0.4 pad_maximum_fusion
  206.2 0.1 copy.18
  206.3 39.8 %while.15 = (s32[]{:T(128)}, f32[2,4,384]{2,1,0:T(4,128)S(1)}, f32[2,4,384]{2,1,0:T(4,128)S(1)}, f32[2,4,384,128]{3,2,1,0:T(8,128)}, s32[3,512]{1,0:T(4,128)S(1)...) while((s32[]{:T(128)}, f32[2,4,384]{2,1,0:T(4,128)S(1)}, ...), condition=%wide.region_4.5_spmd.clone, body=%wide.region_1.0_spmd.clone.sunk | while | flops 827538432 | bytes 50543788 | solution.py:105
  206.3 0.2 compare_and_fusion.2
  206.6 0.4 constant_dynamic-slice_fusion.7
  206.9 3.8 %fusion.37 = (f32[2,4,384]{2,1,0:T(4,128)S(1)}, f32[2,512,384,4]{2,1,3,0:T(8,128)}) fusion(pred[384,512]{0,1:T(8,128)(4,1)S(1)} %compare_and_fusion.2, bf16[384,2,4,128]{3,0,2,1:T(8,128)(2,1)S(1)} %get-tuple-element.281, bf16[1,512,2,128]{3,2,1,0:T(2,128)(2,1)S(1)} %get-tuple-element.240), kind=kOutput, calls=%fused_computation.3.clone.1 | convolution fusion | flops 407368704 | bytes 7548928 | tf_op jit(solution)/shard_map/while/body/eval_jaxpr/tkgd,nkd->kgtn/dot_general | solution.py:88
  210.8 0.0 copy-start.1
  210.8 4.4 %fusion.38 = f32[2,4,384]{2,1,0:T(4,128)S(1)} fusion(f32[2,512,384,4]{2,1,3,0:T(8,128)} %get-tuple-element.242, f32[2,4,384]{2,1,0:T(4,128)S(1)} %select_maximum_fusion.2, pred[384,512]{0,1:T(8,128)(4,1)S(1)} %compare_and_fusion.2), kind=kLoop, calls=%fused_computation.5.clone.1 | loop fusion | flops 7861248 | bytes 6512640 | tf_op jit(solution)/shard_map/while/body/eval_jaxpr/reduce_sum | solution.py:95
  215.3 0.1 copy-done.1
  215.4 3.4 %fusion.40 = f32[2,4,384,128]{3,2,1,0:T(8,128)} fusion(f32[2,4,384,128]{3,2,1,0:T(8,128)} %get-tuple-element.262, f32[2,512,384,4]{2,1,3,0:T(8,128)S(1)} %copy-done.1, f32[2,4,384]{2,1,0:T(4,128)S(1)} %select_maximum_fusion.2, pred[384,512]{0,1:T(8,128)(4,1)S(1)} %compare_and_fusion.2, f32[2,4,384]{2,1,0:T(4,128)S(1)} %get-tuple-element.244, ...), kind=kOutput, calls=%fused_computation.9.clone.1 | convolution fusion | flops 411697152 | bytes 9920513 | tf_op jit(solution)/shard_map/while/body/eval_jaxpr/kgtn,nkd->kgtd/dot_general | solution.py:96
  218.8 0.2 compare_and_fusion.2
  219.1 0.4 constant_dynamic-slice_fusion.7
  219.4 3.9 %fusion.37 = (f32[2,4,384]{2,1,0:T(4,128)S(1)}, f32[2,512,384,4]{2,1,3,0:T(8,128)}) fusion(pred[384,512]{0,1:T(8,128)(4,1)S(1)} %compare_and_fusion.2, bf16[384,2,4,128]{3,0,2,1:T(8,128)(2,1)S(1)} %get-tuple-element.281, bf16[1,512,2,128]{3,2,1,0:T(2,128)(2,1)S(1)} %get-tuple-element.240), kind=kOutput, calls=%fused_computation.3.clone.1 | convolution fusion | flops 407368704 | bytes 7548928 | tf_op jit(solution)/shard_map/while/body/eval_jaxpr/tkgd,nkd->kgtn/dot_general | solution.py:88
  223.3 0.0 copy-start.1
  223.3 4.4 %fusion.38 = f32[2,4,384]{2,1,0:T(4,128)S(1)} fusion(f32[2,512,384,4]{2,1,3,0:T(8,128)} %get-tuple-element.242, f32[2,4,384]{2,1,0:T(4,128)S(1)} %select_maximum_fusion.2, pred[384,512]{0,1:T(8,128)(4,1)S(1)} %compare_and_fusion.2), kind=kLoop, calls=%fused_computation.5.clone.1 | loop fusion | flops 7861248 | bytes 6512640 | tf_op jit(solution)/shard_map/while/body/eval_jaxpr/reduce_sum | solution.py:95
  227.8 0.1 copy-done.1
  227.9 4.6 %fusion.40 = f32[2,4,384,128]{3,2,1,0:T(8,128)} fusion(f32[2,4,384,128]{3,2,1,0:T(8,128)} %get-tuple-element.262, f32[2,512,384,4]{2,1,3,0:T(8,128)S(1)} %copy-done.1, f32[2,4,384]{2,1,0:T(4,128)S(1)} %select_maximum_fusion.2, pred[384,512]{0,1:T(8,128)(4,1)S(1)} %compare_and_fusion.2, f32[2,4,384]{2,1,0:T(4,128)S(1)} %get-tuple-element.244, ...), kind=kOutput, calls=%fused_computation.9.clone.1 | convolution fusion | flops 411697152 | bytes 9920513 | tf_op jit(solution)/shard_map/while/body/eval_jaxpr/kgtn,nkd->kgtd/dot_general | solution.py:96
  232.5 0.2 compare_and_fusion.2
  232.7 0.4 constant_dynamic-slice_fusion.7
  233.1 3.8 %fusion.37 = (f32[2,4,384]{2,1,0:T(4,128)S(1)}, f32[2,512,384,4]{2,1,3,0:T(8,128)}) fusion(pred[384,512]{0,1:T(8,128)(4,1)S(1)} %compare_and_fusion.2, bf16[384,2,4,128]{3,0,2,1:T(8,128)(2,1)S(1)} %get-tuple-element.281, bf16[1,512,2,128]{3,2,1,0:T(2,128)(2,1)S(1)} %get-tuple-element.240), kind=kOutput, calls=%fused_computation.3.clone.1 | convolution fusion | flops 407368704 | bytes 7548928 | tf_op jit(solution)/shard_map/while/body/eval_jaxpr/tkgd,nkd->kgtn/dot_general | solution.py:88
  236.9 0.0 copy-start.1
  236.9 4.4 %fusion.38 = f32[2,4,384]{2,1,0:T(4,128)S(1)} fusion(f32[2,512,384,4]{2,1,3,0:T(8,128)} %get-tuple-element.242, f32[2,4,384]{2,1,0:T(4,128)S(1)} %select_maximum_fusion.2, pred[384,512]{0,1:T(8,128)(4,1)S(1)} %compare_and_fusion.2), kind=kLoop, calls=%fused_computation.5.clone.1 | loop fusion | flops 7861248 | bytes 6512640 | tf_op jit(solution)/shard_map/while/body/eval_jaxpr/reduce_sum | solution.py:95
  241.4 0.1 copy-done.1
  241.5 4.6 %fusion.40 = f32[2,4,384,128]{3,2,1,0:T(8,128)} fusion(f32[2,4,384,128]{3,2,1,0:T(8,128)} %get-tuple-element.262, f32[2,512,384,4]{2,1,3,0:T(8,128)S(1)} %copy-done.1, f32[2,4,384]{2,1,0:T(4,128)S(1)} %select_maximum_fusion.2, pred[384,512]{0,1:T(8,128)(4,1)S(1)} %compare_and_fusion.2, f32[2,4,384]{2,1,0:T(4,128)S(1)} %get-tuple-element.244, ...), kind=kOutput, calls=%fused_computation.9.clone.1 | convolution fusion | flops 411697152 | bytes 9920513 | tf_op jit(solution)/shard_map/while/body/eval_jaxpr/kgtn,nkd->kgtd/dot_general | solution.py:96
  246.1 1.9 fusion.17
  248.0 0.6 copy.21
  248.6 1.4 convert_element_type.46
  (27 shorter events, 0.3 us)
Async XLA Ops:
  6.5 3.2 %copy-start = (s32[1536]{0:T(1024)S(1)}, s32[1536]{0:T(1024)}, u32[]{:S(2)}) copy-start(s32[1536]{0:T(1024)} %param.15) | copy-start | bytes 18436
  6.5 2.2 copy-start.3
  6.5 3.1 %copy-start.2 = (bf16[8192]{0:T(1024)(128)(2,1)S(1)}, bf16[8192]{0:T(1024)(128)(2,1)}, u32[]{:S(2)}) copy-start(bf16[8192]{0:T(1024)(128)(2,1)} %param.10) | copy-start | bytes 49156
  6.5 39.6 %all-gather.4.cloned.1.call-start = ((), (), s32[]{:S(2)}) async-start(), calls=%async_computation | async-start | bytes 5242880 | tf_op jit(solution)/shard_map/all_gather | solution.py:46
  7.3 77.5 %all-gather.8.cloned.1.call-start = ((), (), s32[]{:S(2)}) async-start(), calls=%async_computation.2 | async-start | bytes 5242880 | tf_op jit(solution)/shard_map/all_gather | solution.py:50
  8.0 184.3 %all-gather.6.cloned.1.call-start = ((), (), s32[]{:S(2)}) async-start(), calls=%async_computation.1 | async-start | bytes 20971520 | tf_op jit(solution)/shard_map/all_gather | solution.py:42
  210.8 4.6 %copy-start.1 = (f32[2,512,384,4]{2,1,3,0:T(8,128)S(1)}, f32[2,512,384,4]{2,1,3,0:T(8,128)}, u32[]{:S(2)}) copy-start(f32[2,512,384,4]{2,1,3,0:T(8,128)} %get-tuple-element.242) | copy-start | bytes 18874372 | tf_op jit(solution)/shard_map/while
  223.3 4.6 %copy-start.1 = (f32[2,512,384,4]{2,1,3,0:T(8,128)S(1)}, f32[2,512,384,4]{2,1,3,0:T(8,128)}, u32[]{:S(2)}) copy-start(f32[2,512,384,4]{2,1,3,0:T(8,128)} %get-tuple-element.242) | copy-start | bytes 18874372 | tf_op jit(solution)/shard_map/while
  236.9 4.6 %copy-start.1 = (f32[2,512,384,4]{2,1,3,0:T(8,128)S(1)}, f32[2,512,384,4]{2,1,3,0:T(8,128)}, u32[]{:S(2)}) copy-start(f32[2,512,384,4]{2,1,3,0:T(8,128)} %get-tuple-element.242) | copy-start | bytes 18874372 | tf_op jit(solution)/shard_map/while
Sparse Core Ops, SparseCore 0:
  8.9 37.1 all-gather.3
  47.7 37.0 all-gather.7
  86.4 105.9 all-gather.5
where the time goes:
time: 257 us
  waiting for transfers between devices  137 us (53%)
  matrix products  48.9 us (19%)
  other arithmetic  22.9 us (9%)
  blocking collectives  20.7 us (8%)
  between operations  13.3 us (5%)
  local copies, waits for them, and re-layouts  13.2 us (5%)
    all_gather x1, waiting for transfers between devices, local(): lax.all_gather(w_query, 'ctx', axis=0, tiled=True)  92.7 us
    all_gather x1, waiting for transfers between devices, local(): lax.all_gather(w_key, 'ctx', axis=0, tiled=True)  22.8 us
    all_gather x1, waiting for transfers between devices, local(): lax.all_gather(value_weight, 'ctx', axis=0, tiled=True)  19.7 us
    reduce_sum x3, other arithmetic, advance(): new_sum = running_sum * factor + jnp.sum(exps, axis=-1)  13.3 us
    dot_general x3, matrix products, advance(): jnp.einsum('kgtn,nkd->kgtd', exps.astype(jnp.bfloat16), value_block, pref...  12.5 us
    dot_general x1, matrix products, local(): jnp.dot(normed, lax.all_gather(w_query, 'ctx', axis=0, tiled=True), prefe...  12.4 us
    all_gather x1, blocking collectives, local(): key_piece = lax.all_gather(key_rotary, 'ctx', axis=0, tiled=True)  11.9 us
    dot_general x3, matrix products, advance(): jnp.einsum('tkgd,nkd->kgtn', query_rot, key_block, preferred_element_type...  11.5 us
  transfers between devices with their start and end apart: 3, of which 3 were waited for; matrix products, arithmetic and copies ran while one was open for 11% of the time, Pallas kernels for 0%

commit v1 on v0

--- a/solution.py
+++ b/solution.py
@@ -68,8 +68,12 @@
         jnp.zeros((kv_here, group_width, tok_rows, head_size), jnp.float32),
     )
     state = start_state
-    key_piece = lax.all_gather(key_rotary, "ctx", axis=0, tiled=True)
-    value_piece = lax.all_gather(value_b, "ctx", axis=0, tiled=True)
+    read_roots = lambda xx, buf: jnp.split(
+        lax.all_gather(jnp.concatenate([xx, buf], axis=1), "ctx", axis=0, tiled=True),
+        [xx.shape[1]],
+        axis=1,
+    )
+    key_piece, value_piece = read_roots(key_rotary, value_b)
     piece_rows = key_piece.shape[0]
     block_rows = math.gcd(piece_rows, 1024)
     block_count = piece_rows // block_rows

time: 257 us -> 277 us (1.078)
  waiting for transfers between devices: 137 us -> 176 us
  blocking collectives: 20.7 us -> 0 us
  local copies, waits for them, and re-layouts: 13.2 us -> 16.7 us
    all_gather x2 -> x0, blocking collectives: 20.7 us -> none  [the longest x1 11.9 us: local(): key_piece = lax.all_gather(key_rotary, 'ctx', axis=0, tiled=True)]
    all_gather x0 -> x1, waiting for transfers between devices: none -> 10.2 us  [local(): lax.all_gather(jnp.concatenate([xx, buf], axis=1), 'ctx', axis=0, tiled=T...]
    all_gather x1, waiting for transfers between devices: 92.7 us -> 102 us  [local(): lax.all_gather(w_query, 'ctx', axis=0, tiled=True)]
    all_gather x1, waiting for transfers between devices: 19.7 us -> 29.4 us  [local(): lax.all_gather(value_weight, 'ctx', axis=0, tiled=True)]
    all_gather x1, waiting for transfers between devices: 22.8 us -> 32 us  [local(): lax.all_gather(w_key, 'ctx', axis=0, tiled=True)]
  transfers between devices with their start and end apart: 3 -> 4, of which waited for: 3 -> 4; matrix products, arithmetic and copies ran while one was open for 11% -> 10% of each run, Pallas kernels for 0% -> 0%
where the time goes in v1:
time: 277 us
  waiting for transfers between devices  176 us (64%)
  matrix products  47.6 us (17%)
  other arithmetic  22.8 us (8%)
  local copies, waits for them, and re-layouts  16.7 us (6%)
  between operations  13.3 us (5%)
    all_gather x1, waiting for transfers between devices, local(): lax.all_gather(w_query, 'ctx', axis=0, tiled=True)  102 us
    all_gather x1, waiting for transfers between devices, local(): lax.all_gather(w_key, 'ctx', axis=0, tiled=True)  32 us
    all_gather x1, waiting for transfers between devices, local(): lax.all_gather(value_weight, 'ctx', axis=0, tiled=True)  29.4 us
    reduce_sum x3, other arithmetic, advance(): new_sum = running_sum * factor + jnp.sum(exps, axis=-1)  13.4 us
    dot_general x1, matrix products, local(): jnp.dot(normed, lax.all_gather(w_query, 'ctx', axis=0, tiled=True), prefe...  12.2 us
    dot_general x3, matrix products, advance(): jnp.einsum('tkgd,nkd->kgtn', query_rot, key_block, preferred_element_type...  11.4 us
    dot_general x3, matrix products, advance(): jnp.einsum('kgtn,nkd->kgtd', exps.astype(jnp.bfloat16), value_block, pref...  10.8 us
    all_gather x1, waiting for transfers between devices, local(): lax.all_gather(jnp.concatenate([xx, buf], axis=1), 'ctx', axis=0, tiled=T...  10.2 us
  transfers between devices with their start and end apart: 4, of which 4 were waited for; matrix products, arithmetic and copies ran while one was open for 10% of the time, Pallas kernels for 0%

profile of v1, /device:TPU:0, one launch (start us, length us, event | category | flops | bytes accessed | tf_op | source)
XLA Modules:
  0.0 276.6 jit_solution(157070263941900255)
XLA Ops:
  6.5 0.0 copy-start
  6.5 0.0 all-gather.5.cloned.1.call-start
  6.5 0.7 all-gather.5.cloned.1.call-update
  7.3 0.0 all-gather.7.cloned.1.call-start
  7.3 0.7 all-gather.7.cloned.1.call-update
  8.0 0.0 all-gather.9.cloned.1.call-start
  8.1 0.7 broadcast_multiply_fusion
  8.7 0.1 fusion.25
  8.8 0.7 convert_element_type.38
  9.5 0.1 fusion.30
  9.6 4.1 %fusion.20 = f32[384]{0:T(512)S(1)} fusion(bf16[384,8192]{1,0:T(8,128)(2,1)} %param.9), kind=kLoop, calls=%fused_computation.29 | loop fusion | flops 9436800 | bytes 6292992 | tf_op jit(solution)/shard_map/reduce_sum | solution.py:36
  13.7 0.4 multiply_cosine_fusion
  14.2 32.0 %all-gather.5.cloned.1.call-done = bf16[8192,256]{1,0:T(8,128)(2,1)} async-done(((bf16[2048,256]{1,0:T(8,128)(2,1)}), bf16[8192,256]{1,0:T(8,128)(2,1)}) %all-gather.5.cloned.1.call-update) | async-done | bytes 4194320 | tf_op jit(solution)/shard_map/all_gather | solution.py:46
  46.1 6.6 %fusion.28 = f32[384,256]{0,1:T(8,128)S(1)} fusion(bf16[8192,256]{1,0:T(8,128)(2,1)} %all-gather.5.cloned.1.call-done, bf16[384,8192]{1,0:T(8,128)(2,1)} %param.9, f32[8192]{0:T(1024)S(1)} %convert_element_type.38, f32[384]{0:T(512)S(1)} %add_rsqrt_fusion), kind=kOutput, calls=%fused_computation.57 | convolution fusion | flops 1623195648 | bytes 10913280 | tf_op jit(solution)/shard_map/dot_general | solution.py:45
  52.7 0.1 subtract_convert_fusion.1
  52.8 29.4 %all-gather.7.cloned.1.call-done = bf16[8192,256]{1,0:T(8,128)(2,1)} async-done(((bf16[2048,256]{1,0:T(8,128)(2,1)}), bf16[8192,256]{1,0:T(8,128)(2,1)}) %all-gather.7.cloned.1.call-update) | async-done | bytes 4194320 | tf_op jit(solution)/shard_map/all_gather | solution.py:50
  82.2 6.6 %convolution_convert_fusion = bf16[384,256]{0,1:T(8,128)(2,1)S(1)} fusion(bf16[8192,256]{1,0:T(8,128)(2,1)} %all-gather.7.cloned.1.call-done, bf16[384,8192]{1,0:T(8,128)(2,1)} %param.9, f32[8192]{0:T(1024)S(1)} %convert_element_type.38, f32[384]{0:T(512)S(1)} %add_rsqrt_fusion), kind=kOutput, calls=%fused_computation.36 | convolution fusion | flops 1623293952 | bytes 10716672 | tf_op jit(solution)/shard_map/dot_general | solution.py:48
  88.8 0.8 pad_maximum_fusion.1
  89.6 0.0 all-gather.9.cloned.1.call-update
  89.6 0.0 all-gather.11.cloned.1.call-start
  89.7 0.5 all-gather.11.cloned.1.call-update
  90.2 0.1 copy.17
  90.3 0.1 copy.18
  90.6 0.0 copy-done
  90.6 8.6 %gather_fusion = s32[1536]{0:T(1024)S(1)} fusion(s32[1536]{0:T(1024)S(1)} %copy-done, s32[2048]{0:T(1024)S(1)} %pad_clamp_fusion), kind=kCustom, calls=%fused_computation | custom fusion | bytes 18432 | tf_op jit(solution)/shard_map/jit(_take)/gather | solution.py:32
  99.2 0.1 dynamic-slice_select_fusion
  99.3 10.2 %all-gather.9.cloned.1.call-done = bf16[1536,512]{0,1:T(8,128)(2,1)} async-done(((bf16[384,512]{0,1:T(8,128)(2,1)}), bf16[1536,512]{0,1:T(8,128)(2,1)}) %all-gather.9.cloned.1.call-update) | async-done | bytes 1572880 | tf_op jit(solution)/shard_map/all_gather | solution.py:72
  109.5 1.5 fusion.31
  110.9 0.6 reshape.201
  111.5 0.8 copy.21
  112.3 0.6 reshape.202
  112.9 1.5 copy.22
  114.4 102.4 %all-gather.11.cloned.1.call-done = bf16[8192,1024]{1,0:T(8,128)(2,1)} async-done(((bf16[2048,1024]{1,0:T(8,128)(2,1)}), bf16[8192,1024]{1,0:T(8,128)(2,1)}) %all-gather.11.cloned.1.call-update) | async-done | bytes 16777232 | tf_op jit(solution)/shard_map/all_gather | solution.py:42
  216.8 12.2 %convolution_bitcast_fusion = f32[48,8,8,128]{3,1,2,0:T(8,128)S(1)} fusion(bf16[8192,1024]{1,0:T(8,128)(2,1)} %all-gather.11.cloned.1.call-done, bf16[384,8192]{1,0:T(8,128)(2,1)} %param.9, f32[8192]{0:T(1024)S(1)} %convert_element_type.38, f32[384]{0:T(512)S(1)} %add_rsqrt_fusion), kind=kOutput, calls=%fused_computation.35 | convolution fusion | flops 6455033856 | bytes 24675840 | tf_op jit(solution)/shard_map/dot_general | solution.py:40
  229.1 0.0 copy-start.2
  229.1 0.3 copy.32
  229.4 0.7 subtract_convert_fusion
  230.1 0.4 pad_maximum_fusion
  230.6 0.1 copy.19
  230.7 0.0 copy-done.2
  230.7 36.8 %while.15 = (s32[]{:T(128)}, f32[2,4,384]{2,1,0:T(4,128)S(1)}, f32[2,4,384]{2,1,0:T(4,128)S(1)}, f32[2,4,384,128]{3,2,1,0:T(8,128)S(1)}, s32[3,512]{1,0:T(4,128)...) while((s32[]{:T(128)}, f32[2,4,384]{2,1,0:T(4,128)S(1)}, ...), condition=%wide.region_4.5_spmd.clone, body=%wide.region_1.0_spmd.clone.sunk | while | flops 827538432 | bytes 49495724 | solution.py:109
  230.7 0.2 compare_and_fusion.2
  231.0 3.8 %fusion.46 = (f32[2,4,384]{2,1,0:T(4,128)S(1)}, f32[2,512,384,4]{2,1,3,0:T(8,128)}) fusion(pred[384,512]{0,1:T(8,128)(4,1)S(1)} %compare_and_fusion.2, bf16[384,2,4,128]{3,0,2,1:T(8,128)(2,1)S(1)} %get-tuple-element.277, bf16[3,512,2,128]{3,1,2,0:T(8,128)(2,1)S(1)} %get-tuple-element.276, s32[]{:T(128)} %get-tuple-element.255), kind=kOutput, calls=%fused_computation.3.clone.1 | convolution fusion | flops 407368704 | bytes 7548932 | tf_op jit(solution)/shard_map/while/body/eval_jaxpr/tkgd,nkd->kgtn/dot_general | solution.py:92
  234.7 0.0 copy-start.1
  234.8 4.5 %fusion.47 = f32[2,4,384]{2,1,0:T(4,128)S(1)} fusion(f32[2,512,384,4]{2,1,3,0:T(8,128)} %get-tuple-element.239, f32[2,4,384]{2,1,0:T(4,128)S(1)} %select_maximum_fusion.2, pred[384,512]{0,1:T(8,128)(4,1)S(1)} %compare_and_fusion.2), kind=kLoop, calls=%fused_computation.5.clone.1 | loop fusion | flops 7861248 | bytes 6512640 | tf_op jit(solution)/shard_map/while/body/eval_jaxpr/reduce_sum | solution.py:99
  239.2 0.1 copy-done.1
  239.3 3.6 %fusion.49 = f32[2,4,384,128]{3,2,1,0:T(8,128)S(1)} fusion(f32[2,4,384,128]{3,2,1,0:T(8,128)S(1)} %get-tuple-element.258, f32[2,512,384,4]{2,1,3,0:T(8,128)S(1)} %copy-done.1, f32[2,4,384]{2,1,0:T(4,128)S(1)} %select_maximum_fusion.2, pred[384,512]{0,1:T(8,128)(4,1)S(1)} %compare_and_fusion.2, f32[2,4,384]{2,1,0:T(4,128)S(1)} %get-tuple-element.241, ...), kind=kOutput, calls=%fused_computation.9.clone.1 | convolution fusion | flops 411697152 | bytes 9921025 | tf_op jit(solution)/shard_map/while/body/eval_jaxpr/kgtn,nkd->kgtd/dot_general | solution.py:100
  243.0 0.2 compare_and_fusion.2
  243.2 3.8 %fusion.46 = (f32[2,4,384]{2,1,0:T(4,128)S(1)}, f32[2,512,384,4]{2,1,3,0:T(8,128)}) fusion(pred[384,512]{0,1:T(8,128)(4,1)S(1)} %compare_and_fusion.2, bf16[384,2,4,128]{3,0,2,1:T(8,128)(2,1)S(1)} %get-tuple-element.277, bf16[3,512,2,128]{3,1,2,0:T(8,128)(2,1)S(1)} %get-tuple-element.276, s32[]{:T(128)} %get-tuple-element.255), kind=kOutput, calls=%fused_computation.3.clone.1 | convolution fusion | flops 407368704 | bytes 7548932 | tf_op jit(solution)/shard_map/while/body/eval_jaxpr/tkgd,nkd->kgtn/dot_general | solution.py:92
  247.0 0.0 copy-start.1
  247.0 4.5 %fusion.47 = f32[2,4,384]{2,1,0:T(4,128)S(1)} fusion(f32[2,512,384,4]{2,1,3,0:T(8,128)} %get-tuple-element.239, f32[2,4,384]{2,1,0:T(4,128)S(1)} %select_maximum_fusion.2, pred[384,512]{0,1:T(8,128)(4,1)S(1)} %compare_and_fusion.2), kind=kLoop, calls=%fused_computation.5.clone.1 | loop fusion | flops 7861248 | bytes 6512640 | tf_op jit(solution)/shard_map/while/body/eval_jaxpr/reduce_sum | solution.py:99
  251.5 0.1 copy-done.1
  251.6 3.6 %fusion.49 = f32[2,4,384,128]{3,2,1,0:T(8,128)S(1)} fusion(f32[2,4,384,128]{3,2,1,0:T(8,128)S(1)} %get-tuple-element.258, f32[2,512,384,4]{2,1,3,0:T(8,128)S(1)} %copy-done.1, f32[2,4,384]{2,1,0:T(4,128)S(1)} %select_maximum_fusion.2, pred[384,512]{0,1:T(8,128)(4,1)S(1)} %compare_and_fusion.2, f32[2,4,384]{2,1,0:T(4,128)S(1)} %get-tuple-element.241, ...), kind=kOutput, calls=%fused_computation.9.clone.1 | convolution fusion | flops 411697152 | bytes 9921025 | tf_op jit(solution)/shard_map/while/body/eval_jaxpr/kgtn,nkd->kgtd/dot_general | solution.py:100
  255.2 0.2 compare_and_fusion.2
  255.5 3.8 %fusion.46 = (f32[2,4,384]{2,1,0:T(4,128)S(1)}, f32[2,512,384,4]{2,1,3,0:T(8,128)}) fusion(pred[384,512]{0,1:T(8,128)(4,1)S(1)} %compare_and_fusion.2, bf16[384,2,4,128]{3,0,2,1:T(8,128)(2,1)S(1)} %get-tuple-element.277, bf16[3,512,2,128]{3,1,2,0:T(8,128)(2,1)S(1)} %get-tuple-element.276, s32[]{:T(128)} %get-tuple-element.255), kind=kOutput, calls=%fused_computation.3.clone.1 | convolution fusion | flops 407368704 | bytes 7548932 | tf_op jit(solution)/shard_map/while/body/eval_jaxpr/tkgd,nkd->kgtn/dot_general | solution.py:92
  259.3 0.0 copy-start.1
  259.3 4.5 %fusion.47 = f32[2,4,384]{2,1,0:T(4,128)S(1)} fusion(f32[2,512,384,4]{2,1,3,0:T(8,128)} %get-tuple-element.239, f32[2,4,384]{2,1,0:T(4,128)S(1)} %select_maximum_fusion.2, pred[384,512]{0,1:T(8,128)(4,1)S(1)} %compare_and_fusion.2), kind=kLoop, calls=%fused_computation.5.clone.1 | loop fusion | flops 7861248 | bytes 6512640 | tf_op jit(solution)/shard_map/while/body/eval_jaxpr/reduce_sum | solution.py:99
  263.8 0.1 copy-done.1
  263.9 3.6 %fusion.49 = f32[2,4,384,128]{3,2,1,0:T(8,128)S(1)} fusion(f32[2,4,384,128]{3,2,1,0:T(8,128)S(1)} %get-tuple-element.258, f32[2,512,384,4]{2,1,3,0:T(8,128)S(1)} %copy-done.1, f32[2,4,384]{2,1,0:T(4,128)S(1)} %select_maximum_fusion.2, pred[384,512]{0,1:T(8,128)(4,1)S(1)} %compare_and_fusion.2, f32[2,4,384]{2,1,0:T(4,128)S(1)} %get-tuple-element.241, ...), kind=kOutput, calls=%fused_computation.9.clone.1 | convolution fusion | flops 411697152 | bytes 9921025 | tf_op jit(solution)/shard_map/while/body/eval_jaxpr/kgtn,nkd->kgtd/dot_general | solution.py:100
  267.5 0.5 fusion.23
  268.0 0.6 copy.23
  268.6 1.4 convert_element_type.46
  (25 shorter events, 0.3 us)
Async XLA Ops:
  6.5 84.0 %copy-start = (s32[1536]{0:T(1024)S(1)}, s32[1536]{0:T(1024)}, u32[]{:S(2)}) copy-start(s32[1536]{0:T(1024)} %param.15) | copy-start | bytes 18436
  6.5 39.6 %all-gather.5.cloned.1.call-start = ((), (), s32[]{:S(2)}) async-start(), calls=%async_computation | async-start | bytes 5242880 | tf_op jit(solution)/shard_map/all_gather | solution.py:46
  7.3 74.9 %all-gather.7.cloned.1.call-start = ((), (), s32[]{:S(2)}) async-start(), calls=%async_computation.1 | async-start | bytes 5242880 | tf_op jit(solution)/shard_map/all_gather | solution.py:50
  8.0 101.4 %all-gather.9.cloned.1.call-start = ((), (), s32[]{:S(2)}) async-start(), calls=%async_computation.2 | async-start | bytes 1966080 | tf_op jit(solution)/shard_map/all_gather | solution.py:72
  89.6 127.2 %all-gather.11.cloned.1.call-start = ((), (), s32[]{:S(2)}) async-start(), calls=%async_computation.3 | async-start | bytes 20971520 | tf_op jit(solution)/shard_map/all_gather | solution.py:42
  229.1 1.6 copy-start.2
  234.7 4.6 %copy-start.1 = (f32[2,512,384,4]{2,1,3,0:T(8,128)S(1)}, f32[2,512,384,4]{2,1,3,0:T(8,128)}, u32[]{:S(2)}) copy-start(f32[2,512,384,4]{2,1,3,0:T(8,128)} %get-tuple-element.239) | copy-start | bytes 18874372 | tf_op jit(solution)/shard_map/while
  247.0 4.6 %copy-start.1 = (f32[2,512,384,4]{2,1,3,0:T(8,128)S(1)}, f32[2,512,384,4]{2,1,3,0:T(8,128)}, u32[]{:S(2)}) copy-start(f32[2,512,384,4]{2,1,3,0:T(8,128)} %get-tuple-element.239) | copy-start | bytes 18874372 | tf_op jit(solution)/shard_map/while
  259.3 4.6 %copy-start.1 = (f32[2,512,384,4]{2,1,3,0:T(8,128)S(1)}, f32[2,512,384,4]{2,1,3,0:T(8,128)}, u32[]{:S(2)}) copy-start(f32[2,512,384,4]{2,1,3,0:T(8,128)} %get-tuple-element.239) | copy-start | bytes 18874372 | tf_op jit(solution)/shard_map/while
Sparse Core Ops, SparseCore 0:
  8.9 37.1 all-gather.4
  47.7 34.4 all-gather.6
  89.7 19.6 all-gather.8
  110.9 105.9 all-gather.10
